TPU v7x, 32 devices: a whole 2x2x4 slice. The times are simulated.
32 devices in a mesh: term: 4 (over y, x), sector: 8 (over z, core).
Axes of the slice: x: 2, y: 2, z: 4, core: 2. Of those that a mesh axis runs over, the one named last changes fastest.
Arguments:
- psi: bfloat16 [8, 8, 128, 128], P('sector'), may hold values from -6 to 6
- left_env: bfloat16 [8, 8, 128, 128], P('term', 'sector'), may hold values from -40 to 40
- right_env: bfloat16 [8, 8, 128, 128], P('term', 'sector'), may hold values from -4 to 4
- precond: bfloat16 [8, 8, 128, 128], P('sector'), may hold values from 0.5 to 4
- block_sizes: int32 [8], replicated, may hold values from 32 to 128, as said below
Outputs:
- state: bfloat16 [8, 8, 128, 128], P('sector')
- energy: float32 [3], replicated
Inputs may be any that keep to these rules, and one draw needn't show every extreme that they name: `block_sizes`: some sector has exactly 128 rows in every draw.
All inputs are finite; a program needn't handle non-finite values.
Results may differ from a plain program's by a relative error of at most 0.022.
Values may be sent and summed in bfloat16 or wider, within the bound.
No kernel may reach another device: no remote copies, remote signals or barrier semaphores. Data moves between devices by JAX's collectives and lax.ppermute only.
A program may use at most 128 MiB of HBM per device.

v0:
```python
import jax
import jax.numpy as jnp
from jax import lax
from jax.sharding import PartitionSpec as P

ITERS = 3


def block_mask(block_sizes, width, own_row):
    rows = jnp.arange(width)
    valid = rows[None, :] < block_sizes[:, None]
    own_valid = lax.dynamic_slice_in_dim(valid, own_row, 1, 0)[0]
    return (own_valid[None, :, None] & valid[:, None, :]).astype(jnp.float32)


def dot_sums(cur_share, img_share, pre_share, count):
    first = lax.psum(
        (jnp.sum(cur_share * cur_share), jnp.sum(cur_share * img_share)), ("term", "sector")
    )
    theta = first[1] / first[0]
    fresh = cur_share - (img_share - theta * cur_share) / pre_share
    squares = lax.psum(jnp.sum(fresh * fresh), ("term", "sector"))
    return (theta, lax.rsqrt(squares / count + 1e-06))


def local(psi, left_env, right_env, precond, block_sizes):
    sectors = block_sizes.shape[0]
    width = psi.shape[-1]
    own_row = lax.axis_index("sector")
    share = sectors // lax.axis_size("term")
    share_start = lax.axis_index("term") * share
    count = float(sectors * sectors * width * width)
    mask = block_mask(block_sizes, width, own_row)
    state = (psi[0].astype(jnp.float32) * mask).astype(jnp.bfloat16)
    scaling = precond[0].astype(jnp.float32)
    left_own = left_env[:, 0]

    def portion(values):
        return lax.dynamic_slice_in_dim(values, share_start, share, 0)

    right_all = lax.all_gather(right_env, "sector", axis=1, tiled=True)
    energies = []
    for step in range(ITERS):
        images = jnp.einsum(
            "jab,kjcb->kjac", state, right_all, preferred_element_type=jnp.float32
        ).astype(jnp.bfloat16)
        partial_value = jnp.einsum(
            "kac,kjcd->jad", left_own, images, preferred_element_type=jnp.float32
        )
        current = state.astype(jnp.float32)
        image = lax.psum(partial_value.astype(jnp.bfloat16), "term").astype(jnp.float32) * mask
        theta, factor = dot_sums(portion(current), portion(image), portion(scaling), count)
        fresh = current - (image - theta * current) / scaling
        state = (fresh * factor).astype(jnp.bfloat16)
        energies.append(theta)
    return (state[None], jnp.stack(energies))


def solution(mesh):
    in_specs = (
        P("sector", None, None, None),
        P("term", "sector", None, None),
        P("term", "sector", None, None),
        P("sector", None, None, None),
        P(),
    )
    out_specs = (P("sector", None, None, None), P())
    return jax.shard_map(local, mesh=mesh, in_specs=in_specs, out_specs=out_specs, check_vma=False)
```

profile of v0, /device:TPU:0, one launch (start us, length us, event | category | flops | bytes accessed | tf_op | source)
XLA Modules:
  0.0 424.9 jit_solution(16946019127858269423)
XLA Ops:
  7.2 0.6 copy-done.6
  8.0 1.1 copy.7
  9.1 16.6 %all_gather.3 = bf16[2,8,128,128]{3,2,1,0:T(8,128)(2,1)S(1)} all-gather(bf16[2,1,128,128]{3,2,1,0:T(8,128)(2,1)S(1)} %copy-done.5), channel_id=1, replica_groups=mesh['term'=4,'sector'=8] {'sector'}, dimensions={1}, use_global_device_ids=true | all-gather | bytes 589824 | tf_op jit(solution)/shard_map/all_gather | solution.py:41
  25.7 1.2 fusion.8
  27.1 0.9 copy-done.4
  28.1 43.0 %all-reduce.7.cloned.1.call-done = bf16[8,128,128]{1,2,0:T(8,128)(2,1)} async-done(((bf16[8,128,128]{1,2,0:T(8,128)(2,1)}), bf16[8,128,128]{1,2,0:T(8,128)(2,1)}) %all-reduce.7.cloned.1.call-update) | async-done | bytes 262160 | tf_op jit(solution)/shard_map/psum | solution.py:51
  71.1 1.2 fusion.34
  72.3 0.6 multiply_reduce_fusion.4
  72.9 39.6 %all-reduce.2 = (f32[]{:T(128)}, f32[]{:T(128)}) all-reduce(f32[]{:T(128)} %get-tuple-element.9, f32[]{:T(128)} %get-tuple-element.8), channel_id=1, replica_groups=mesh['term'=4,'sector'=8] {'term','sector'}, use_global_device_ids=true, to_apply=%region_2.0 | all-reduce | flops 2 | bytes 16 | tf_op jit(solution)/shard_map/psum | solution.py:17
  113.9 0.7 fusion.43
  114.5 41.4 %psum.87 = f32[]{:T(128)} all-reduce(f32[]{:T(128)} %fusion.43), channel_id=1, replica_groups=mesh['term'=4,'sector'=8] {'term','sector'}, use_global_device_ids=true, to_apply=%region_6.0 | all-reduce | flops 1 | bytes 8 | tf_op jit(solution)/shard_map/psum | solution.py:22
  156.9 1.2 fusion.7
  158.1 43.0 %all-reduce.9.cloned.1.call-done = bf16[8,128,128]{1,2,0:T(8,128)(2,1)} async-done(((bf16[8,128,128]{1,2,0:T(8,128)(2,1)}), bf16[8,128,128]{1,2,0:T(8,128)(2,1)}) %all-reduce.9.cloned.1.call-update) | async-done | bytes 262160 | tf_op jit(solution)/shard_map/psum | solution.py:51
  201.2 1.1 and_select_fusion.1
  203.0 39.6 %all-reduce.1 = (f32[]{:T(128)}, f32[]{:T(128)}) all-reduce(f32[]{:T(128)} %get-tuple-element.7, f32[]{:T(128)} %get-tuple-element.6), channel_id=1, replica_groups=mesh['term'=4,'sector'=8] {'term','sector'}, use_global_device_ids=true, to_apply=%region_9.0 | all-reduce | flops 2 | bytes 16 | tf_op jit(solution)/shard_map/psum | solution.py:17
  243.9 0.7 fusion.42
  244.5 41.4 %psum.91 = f32[]{:T(128)} all-reduce(f32[]{:T(128)} %fusion.42), channel_id=1, replica_groups=mesh['term'=4,'sector'=8] {'term','sector'}, use_global_device_ids=true, to_apply=%region_13.0 | all-reduce | flops 1 | bytes 8 | tf_op jit(solution)/shard_map/psum | solution.py:22
  286.9 1.2 fusion.6
  288.1 43.1 %all-reduce.11.cloned.1.call-done = bf16[8,128,128]{1,2,0:T(8,128)(2,1)} async-done(((bf16[8,128,128]{1,2,0:T(8,128)(2,1)}), bf16[8,128,128]{1,2,0:T(8,128)(2,1)}) %all-reduce.11.cloned.1.call-update) | async-done | bytes 262160 | tf_op jit(solution)/shard_map/psum | solution.py:51
  331.2 1.1 and_select_fusion
  333.0 39.6 %all-reduce = (f32[]{:T(128)}, f32[]{:T(128)}) all-reduce(f32[]{:T(128)} %get-tuple-element.5, f32[]{:T(128)} %get-tuple-element.4), channel_id=1, replica_groups=mesh['term'=4,'sector'=8] {'term','sector'}, use_global_device_ids=true, to_apply=%region_16.0 | all-reduce | flops 2 | bytes 16 | tf_op jit(solution)/shard_map/psum | solution.py:17
  373.9 0.7 fusion.41
  374.5 41.4 %psum.95 = f32[]{:T(128)} all-reduce(f32[]{:T(128)} %fusion.41), channel_id=1, replica_groups=mesh['term'=4,'sector'=8] {'term','sector'}, use_global_device_ids=true, to_apply=%region_20.0 | all-reduce | flops 1 | bytes 8 | tf_op jit(solution)/shard_map/psum | solution.py:22
  416.9 0.9 copy.9
  (28 shorter events, 3.3 us)
Async XLA Ops:
  7.2 18.6 %copy-start = (bf16[2,1,128,128]{3,2,1,0:T(8,128)(2,1)S(1)}, bf16[2,1,128,128]{3,2,1,0:T(8,128)(2,1)}, u32[]{:S(2)}) copy-start(bf16[2,1,128,128]{3,2,1,0:T(8,128)(2,1)} %param.6) | copy-start | bytes 196612
  7.2 64.0 %all-reduce.7.cloned.1.call-start = ((), (), s32[]{:S(2)}) async-start(), calls=%async_computation | async-start | bytes 524288 | tf_op jit(solution)/shard_map/psum | solution.py:51
  7.2 0.7 copy-start.6
  8.0 1.2 copy-start.5
  27.0 0.9 copy-start.4
  27.0 174.2 %all-reduce.9.cloned.1.call-start = ((), (), s32[]{:S(2)}) async-start(), calls=%async_computation.1 | async-start | bytes 524288 | tf_op jit(solution)/shard_map/psum | solution.py:51
  72.9 83.6 %copy-start.1 = (bf16[8,128,128]{1,2,0:T(8,128)(2,1)S(1)}, bf16[8,128,128]{1,2,0:T(8,128)(2,1)}, u32[]{:S(2)}) copy-start(bf16[8,128,128]{1,2,0:T(8,128)(2,1)} %all-reduce.7.cloned.1.call-done) | copy-start | bytes 786436
  158.1 173.1 %all-reduce.11.cloned.1.call-start = ((), (), s32[]{:S(2)}) async-start(), calls=%async_computation.2 | async-start | bytes 524288 | tf_op jit(solution)/shard_map/psum | solution.py:51
  203.0 83.6 %copy-start.3 = (bf16[8,128,128]{1,2,0:T(8,128)(2,1)S(1)}, bf16[8,128,128]{1,2,0:T(8,128)(2,1)}, u32[]{:S(2)}) copy-start(bf16[8,128,128]{1,2,0:T(8,128)(2,1)} %all-reduce.9.cloned.1.call-done) | copy-start | bytes 786436
  333.0 83.6 %copy-start.2 = (bf16[8,128,128]{1,2,0:T(8,128)(2,1)S(1)}, bf16[8,128,128]{1,2,0:T(8,128)(2,1)}, u32[]{:S(2)}) copy-start(bf16[8,128,128]{1,2,0:T(8,128)(2,1)} %all-reduce.11.cloned.1.call-done) | copy-start | bytes 786436
Sparse Core Ops, SparseCore 0:
  27.1 43.9 all-reduce.6
  158.2 42.9 all-reduce.8
  288.2 42.9 all-reduce.10
where the time goes:
time: 426 us; the launch traced here: 425 us
  blocking collectives  259 us (61%)
  waiting for transfers between devices  129 us (30%)
  between operations  20 us (5%)
  other arithmetic  8.96 us (2%)
    psum x3, waiting for transfers between devices, local(): lax.psum(partial_value.astype(jnp.bfloat16), 'term').astype(jnp.float32)  129 us
    psum x3, blocking collectives, dot_sums(): squares = lax.psum(jnp.sum(fresh * fresh), ('term', 'sector'))  124 us
    psum x3, blocking collectives, dot_sums(): lax.psum((jnp.sum(cur_share * cur_share), jnp.sum(cur_share * img_share))...  119 us
    all_gather x1, blocking collectives, local(): right_all = lax.all_gather(right_env, 'sector', axis=1, tiled=True)  16.6 us
  transfers between devices with their start and end apart: 3, of which 3 were waited for; matrix products, arithmetic and copies ran while one was open for 0% of the time, Pallas kernels for 0%

commit v1 on v0

--- a/solution.py
+++ b/solution.py
@@ -48,7 +48,12 @@
             "kac,kjcd->jad", left_own, images, preferred_element_type=jnp.float32
         )
         current = state.astype(jnp.float32)
-        image = lax.psum(partial_value.astype(jnp.bfloat16), "term").astype(jnp.float32) * mask
+        image = (
+            jnp.sum(lax.all_gather(partial_value.astype(jnp.bfloat16), "term"), axis=0).astype(
+                jnp.float32
+            )
+            * mask
+        )
         theta, factor = dot_sums(portion(current), portion(image), portion(scaling), count)
         fresh = current - (image - theta * current) / scaling
         state = (fresh * factor).astype(jnp.bfloat16)

time: 426 us -> 380 us (0.89)
  waiting for transfers between devices: 129 us -> 80 us
    psum x3 -> x0, waiting for transfers between devices: 129 us -> none  [local(): lax.psum(partial_value.astype(jnp.bfloat16), 'term').astype(jnp.float32)]
    all_gather x0 -> x3, waiting for transfers between devices: none -> 79.9 us  [local(): lax.all_gather(partial_value.astype(jnp.bfloat16), 'term')]
where the time goes in v1:
time: 380 us; the launch traced here: 378 us
  blocking collectives  259 us (68%)
  waiting for transfers between devices  80 us (21%)
  between operations  20 us (5%)
  other arithmetic  10.6 us (3%)
  local copies, waits for them, and re-layouts  6.8 us (2%)
    psum x3, blocking collectives, dot_sums(): squares = lax.psum(jnp.sum(fresh * fresh), ('term', 'sector'))  124 us
    psum x3, blocking collectives, dot_sums(): lax.psum((jnp.sum(cur_share * cur_share), jnp.sum(cur_share * img_share))...  119 us
    all_gather x3, waiting for transfers between devices, local(): lax.all_gather(partial_value.astype(jnp.bfloat16), 'term')  79.9 us
    all_gather x1, blocking collectives, local(): right_all = lax.all_gather(right_env, 'sector', axis=1, tiled=True)  16.6 us
  transfers between devices with their start and end apart: 3, of which 3 were waited for; matrix products, arithmetic and copies ran while one was open for 0% of the time, Pallas kernels for 0%

profile of v1, /device:TPU:0, one launch (start us, length us, event | category | flops | bytes accessed | tf_op | source)
XLA Modules:
  0.0 378.4 jit_solution(772260721307751937)
XLA Ops:
  7.2 0.6 copy-done.3
  8.0 1.1 copy.7
  9.1 16.6 %all_gather.21 = bf16[2,8,128,128]{3,2,1,0:T(8,128)(2,1)S(1)} all-gather(bf16[2,1,128,128]{3,2,1,0:T(8,128)(2,1)S(1)} %copy-done.2), channel_id=1, replica_groups=mesh['term'=4,'sector'=8] {'sector'}, dimensions={1}, use_global_device_ids=true | all-gather | bytes 589824 | tf_op jit(solution)/shard_map/all_gather | solution.py:41
  26.3 0.9 copy.8
  27.2 0.9 copy-done.1
  28.3 26.7 %all-gather.7.cloned.1.call-done = bf16[32,128,128]{2,1,0:T(8,128)(2,1)} async-done(((bf16[8,128,128]{2,1,0:T(8,128)(2,1)}), bf16[32,128,128]{2,1,0:T(8,128)(2,1)}) %all-gather.7.cloned.1.call-update) | async-done | bytes 1048592 | tf_op jit(solution)/shard_map/all_gather | solution.py:52
  55.0 1.4 reduce_sum.117
  57.4 39.6 %all-reduce.2 = (f32[]{:T(128)}, f32[]{:T(128)}) all-reduce(f32[]{:T(128)} %get-tuple-element.7, f32[]{:T(128)} %get-tuple-element.6), channel_id=1, replica_groups=mesh['term'=4,'sector'=8] {'term','sector'}, use_global_device_ids=true, to_apply=%region_2.0 | all-reduce | flops 2 | bytes 16 | tf_op jit(solution)/shard_map/psum | solution.py:17
  98.3 0.7 fusion.56
  99.0 41.4 %psum.65 = f32[]{:T(128)} all-reduce(f32[]{:T(128)} %fusion.56), channel_id=1, replica_groups=mesh['term'=4,'sector'=8] {'term','sector'}, use_global_device_ids=true, to_apply=%region_6.0 | all-reduce | flops 1 | bytes 8 | tf_op jit(solution)/shard_map/psum | solution.py:22
  141.8 0.9 copy.11
  142.8 26.7 %all-gather.9.cloned.1.call-done = bf16[32,128,128]{2,1,0:T(8,128)(2,1)} async-done(((bf16[8,128,128]{2,1,0:T(8,128)(2,1)}), bf16[32,128,128]{2,1,0:T(8,128)(2,1)}) %all-gather.9.cloned.1.call-update) | async-done | bytes 1048592 | tf_op jit(solution)/shard_map/all_gather | solution.py:52
  169.5 1.4 reduce_sum.121
  171.9 39.6 %all-reduce.1 = (f32[]{:T(128)}, f32[]{:T(128)}) all-reduce(f32[]{:T(128)} %get-tuple-element.5, f32[]{:T(128)} %get-tuple-element.4), channel_id=1, replica_groups=mesh['term'=4,'sector'=8] {'term','sector'}, use_global_device_ids=true, to_apply=%region_9.0 | all-reduce | flops 2 | bytes 16 | tf_op jit(solution)/shard_map/psum | solution.py:17
  212.8 0.7 fusion.55
  213.5 41.4 %psum.68 = f32[]{:T(128)} all-reduce(f32[]{:T(128)} %fusion.55), channel_id=1, replica_groups=mesh['term'=4,'sector'=8] {'term','sector'}, use_global_device_ids=true, to_apply=%region_13.0 | all-reduce | flops 1 | bytes 8 | tf_op jit(solution)/shard_map/psum | solution.py:22
  256.4 0.9 copy.13
  257.4 26.6 %all-gather.11.cloned.1.call-done = bf16[32,128,128]{2,1,0:T(8,128)(2,1)} async-done(((bf16[8,128,128]{2,1,0:T(8,128)(2,1)}), bf16[32,128,128]{2,1,0:T(8,128)(2,1)}) %all-gather.11.cloned.1.call-update) | async-done | bytes 1048592 | tf_op jit(solution)/shard_map/all_gather | solution.py:52
  284.0 1.4 reduce_sum.125
  285.6 0.7 fusion.48
  286.3 39.6 %all-reduce = (f32[]{:T(128)}, f32[]{:T(128)}) all-reduce(f32[]{:T(128)} %get-tuple-element.9, f32[]{:T(128)} %get-tuple-element.8), channel_id=1, replica_groups=mesh['term'=4,'sector'=8] {'term','sector'}, use_global_device_ids=true, to_apply=%region_16.0 | all-reduce | flops 2 | bytes 16 | tf_op jit(solution)/shard_map/psum | solution.py:17
  327.2 0.7 fusion.46
  327.9 41.4 %psum.71 = f32[]{:T(128)} all-reduce(f32[]{:T(128)} %fusion.46), channel_id=1, replica_groups=mesh['term'=4,'sector'=8] {'term','sector'}, use_global_device_ids=true, to_apply=%region_20.0 | all-reduce | flops 1 | bytes 8 | tf_op jit(solution)/shard_map/psum | solution.py:22
  370.5 0.8 copy.15
  (32 shorter events, 6.2 us)
Async XLA Ops:
  7.2 18.6 %copy-start = (bf16[2,1,128,128]{3,2,1,0:T(8,128)(2,1)S(1)}, bf16[2,1,128,128]{3,2,1,0:T(8,128)(2,1)}, u32[]{:S(2)}) copy-start(bf16[2,1,128,128]{3,2,1,0:T(8,128)(2,1)} %param.6) | copy-start | bytes 196612
  7.2 47.8 %all-gather.7.cloned.1.call-start = ((), (), s32[]{:S(2)}) async-start(), calls=%async_computation | async-start | bytes 1310720 | tf_op jit(solution)/shard_map/all_gather | solution.py:52
  7.2 0.7 copy-start.3
  8.0 1.2 copy-start.2
  27.1 0.9 copy-start.1
  27.1 142.3 %all-gather.9.cloned.1.call-start = ((), (), s32[]{:S(2)}) async-start(), calls=%async_computation.1 | async-start | bytes 1310720 | tf_op jit(solution)/shard_map/all_gather | solution.py:52
  142.7 141.3 %all-gather.11.cloned.1.call-start = ((), (), s32[]{:S(2)}) async-start(), calls=%async_computation.2 | async-start | bytes 1310720 | tf_op jit(solution)/shard_map/all_gather | solution.py:52
Sparse Core Ops, SparseCore 0:
  27.3 27.6 all-gather.6
  142.8 26.6 all-gather.8
  257.3 26.6 all-gather.10
